TPU v7x, 128 devices: a whole 4x4x4 slice. The times are simulated.
128 devices in a mesh: row: 32 (over z, y, core), col: 4 (over x).
Axes of the slice: x: 4, y: 4, z: 4, core: 2. Of those that a mesh axis runs over, the one named last changes fastest.
Arguments:
- positions: bfloat16 [8192, 64], P('row'), as said below
- log_weights: float32 [8192], P('row'), may hold values from 95 to 145
- cotangent: bfloat16 [8192, 64], P('row'), may hold values from -6 to 6
Outputs:
- grad_positions: float32 [8192, 64], P(('row', 'col'))
- grad_log_weights: float32 [8192], P('row')
Inputs may be any that keep to these rules, and one draw needn't show every extreme that they name: `positions`: particle states are finite real vectors.
All inputs are finite; a program needn't handle non-finite values.
Results may differ from a plain program's by a relative error of at most 0.008.
Values may be sent and summed in bfloat16 or wider, within the bound.
No kernel may reach another device: no remote copies, remote signals or barrier semaphores. Data moves between devices by JAX's collectives and lax.ppermute only.
A program may use at most 64 MiB of HBM per device.

v0:
```python
import math

import jax
import jax.numpy as jnp
from jax import lax
from jax.sharding import PartitionSpec as P

ITERS = 5


def row_lse(logits):
    highest = lax.pmax(jnp.max(logits, axis=1), "col")
    total_mass = lax.psum(jnp.sum(jnp.exp(logits - highest[:, None]), axis=1), "col")
    return highest + jnp.log(total_mass)


def column_lse(logits):
    highest = lax.pmax(jnp.max(logits, axis=0), "row")
    total_mass = lax.psum(jnp.sum(jnp.exp(logits - highest[None, :]), axis=0), "row")
    return highest + jnp.log(total_mass)


def local(positions, log_weights, cotangent):
    row_count = positions.shape[0]
    feature_dim = positions.shape[1]
    col_count = lax.axis_size("col")
    piece_len = row_count // col_count
    offset = lax.axis_index("col") * piece_len
    own_pos = lax.dynamic_slice_in_dim(positions, offset, piece_len, 0)
    own_cot = lax.dynamic_slice_in_dim(cotangent, offset, piece_len, 0)
    col_pos, col_cot = (
        lax.all_gather(own_pos, "row", axis=0, tiled=True),
        lax.all_gather(own_cot, "row", axis=0, tiled=True),
    )
    particle_total = col_pos.shape[0] * col_count
    log_count = math.log(particle_total)
    cost_scale = 4.0 / feature_dim
    row_f32 = positions.astype(jnp.float32)
    col_f32 = col_pos.astype(jnp.float32)
    row_sq = jnp.sum(row_f32 * row_f32, axis=1)
    col_sq = jnp.sum(col_f32 * col_f32, axis=1)

    def distances():
        cross = lax.dot_general(
            positions, col_pos, (((1,), (1,)), ((), ())), preferred_element_type=jnp.float32
        )
        return cost_scale * (row_sq[:, None] + col_sq[None, :] - 2.0 * cross)

    col_pot = jnp.zeros((col_pos.shape[0],), jnp.float32)
    rows_saved = []
    cols_saved = [col_pot]
    for section in range(ITERS):
        cost_tile = distances()
        row_pot = log_count - row_lse(col_pot[None, :] - cost_tile)
        col_pot = -column_lse(row_pot[:, None] + log_weights[:, None] - cost_tile)
        rows_saved.append(row_pot)
        cols_saved.append(col_pot)
    cost_tile = distances()
    transport = jnp.exp(
        rows_saved[-1][:, None] + cols_saved[-1][None, :] + log_weights[:, None] - cost_tile
    )
    paired = lax.dot_general(
        positions, col_cot, (((1,), (1,)), ((), ())), preferred_element_type=jnp.float32
    )
    weighted = transport * paired
    gradient_tile = -weighted
    col_grad = lax.psum(jnp.sum(weighted, axis=0), "row")
    surplus = jnp.sum(weighted, axis=1)
    grad_log_weights = jnp.zeros((row_count,), jnp.float32)
    for section in reversed(range(ITERS)):
        if section < ITERS - 1:
            cost_tile = distances()
        upper = rows_saved[section]
        column_soft = jnp.exp(
            upper[:, None] + log_weights[:, None] - cost_tile + cols_saved[section + 1][None, :]
        )
        row_grad = lax.psum(surplus - jnp.sum(column_soft * col_grad[None, :], axis=1), "col")
        surplus = jnp.zeros((row_count,), jnp.float32)
        back_tile = jnp.exp(cols_saved[section][None, :] - cost_tile + upper[:, None] - log_count)
        gradient_tile = (
            gradient_tile + column_soft * col_grad[None, :] + back_tile * row_grad[:, None]
        )
        grad_log_weights = grad_log_weights + row_grad
        if section > 0:
            col_grad = -lax.psum(jnp.sum(back_tile * row_grad[:, None], axis=0), "row")
    row_mass = jnp.sum(gradient_tile, axis=1)
    col_mass = jnp.sum(gradient_tile, axis=0)
    narrow = gradient_tile.astype(jnp.bfloat16)
    direct = jnp.dot(transport.astype(jnp.bfloat16), col_cot, preferred_element_type=jnp.float32)
    pulled = jnp.dot(narrow, col_pos, preferred_element_type=jnp.float32)
    pushed = lax.dot_general(
        narrow, positions, (((0,), (0,)), ((), ())), preferred_element_type=jnp.float32
    )
    row_term = direct + 2.0 * cost_scale * (row_mass[:, None] * row_f32 - pulled)
    col_term = 2.0 * cost_scale * (col_mass[:, None] * col_f32 - pushed)
    row_part = lax.psum_scatter(
        row_term.astype(jnp.bfloat16), "col", scatter_dimension=0, tiled=True
    ).astype(jnp.float32)
    summed = lax.psum(col_term.astype(jnp.bfloat16), "row").astype(jnp.float32)
    col_part = lax.dynamic_slice_in_dim(summed, lax.axis_index("row") * piece_len, piece_len, 0)
    return (row_part + col_part, grad_log_weights)


def solution(mesh):
    in_specs = (P("row", None), P("row"), P("row", None))
    out_specs = (P(("row", "col"), None), P("row"))
    return jax.shard_map(local, mesh=mesh, in_specs=in_specs, out_specs=out_specs, check_vma=False)
```

profile of v0, /device:TPU:1, one launch (start us, length us, event | category | flops | bytes accessed | tf_op | source)
XLA Modules:
  0.0 1291.2 jit_solution(14466195769258401368)
XLA Ops:
  9.3 27.6 %all_gather.6 = bf16[2048,64]{1,0:T(8,128)(2,1)S(1)} all-gather(bf16[64,64]{1,0:T(8,128)(2,1)S(1)} %constant_dynamic-slice_fusion.1), channel_id=1, replica_groups=mesh['row'=32,'col'=4] {'row'}, dimensions={0}, use_global_device_ids=true | all-gather | bytes 270336 | tf_op jit(solution)/shard_map/all_gather | solution.py:32
  37.3 24.2 %all_gather.7 = bf16[2048,64]{1,0:T(8,128)(2,1)S(1)} all-gather(bf16[64,64]{1,0:T(8,128)(2,1)S(1)} %copy.10), channel_id=1, replica_groups=mesh['row'=32,'col'=4] {'row'}, dimensions={0}, use_global_device_ids=true | all-gather | bytes 270336 | tf_op jit(solution)/shard_map/all_gather | solution.py:33
  62.8 8.5 pmax.70
  78.1 66.9 %pmax.71 = f32[2048]{0:T(1024)S(1)} all-reduce(f32[2048]{0:T(1024)S(1)} %subtract_reduce_fusion.8), channel_id=1, replica_groups=mesh['row'=32,'col'=4] {'row'}, use_global_device_ids=true, to_apply=%region_7.0 | all-reduce | flops 2048 | bytes 16384 | tf_op jit(solution)/shard_map/pmax | solution.py:18
  145.7 63.7 %psum.148 = f32[2048]{0:T(1024)S(1)} all-reduce(f32[2048]{0:T(1024)S(1)} %exponential_reduce_fusion.8), channel_id=1, replica_groups=mesh['row'=32,'col'=4] {'row'}, use_global_device_ids=true, to_apply=%region_9.0 | all-reduce | flops 2048 | bytes 16384 | tf_op jit(solution)/shard_map/psum | solution.py:19
  209.8 7.7 pmax.72
  218.0 6.0 psum.149
  224.3 67.4 %pmax.73 = f32[2048]{0:T(1024)S(1)} all-reduce(f32[2048]{0:T(1024)S(1)} %subtract_reduce_fusion.6), channel_id=1, replica_groups=mesh['row'=32,'col'=4] {'row'}, use_global_device_ids=true, to_apply=%region_15.0 | all-reduce | flops 2048 | bytes 16384 | tf_op jit(solution)/shard_map/pmax | solution.py:18
  292.5 63.7 %psum.150 = f32[2048]{0:T(1024)S(1)} all-reduce(f32[2048]{0:T(1024)S(1)} %exponential_reduce_fusion.6), channel_id=1, replica_groups=mesh['row'=32,'col'=4] {'row'}, use_global_device_ids=true, to_apply=%region_17.0 | all-reduce | flops 2048 | bytes 16384 | tf_op jit(solution)/shard_map/psum | solution.py:19
  356.5 7.7 pmax.74
  364.7 6.0 psum.151
  371.1 67.4 %pmax.75 = f32[2048]{0:T(1024)S(1)} all-reduce(f32[2048]{0:T(1024)S(1)} %subtract_reduce_fusion.4), channel_id=1, replica_groups=mesh['row'=32,'col'=4] {'row'}, use_global_device_ids=true, to_apply=%region_23.0 | all-reduce | flops 2048 | bytes 16384 | tf_op jit(solution)/shard_map/pmax | solution.py:18
  439.2 63.7 %psum.152 = f32[2048]{0:T(1024)S(1)} all-reduce(f32[2048]{0:T(1024)S(1)} %exponential_reduce_fusion.4), channel_id=1, replica_groups=mesh['row'=32,'col'=4] {'row'}, use_global_device_ids=true, to_apply=%region_25.0 | all-reduce | flops 2048 | bytes 16384 | tf_op jit(solution)/shard_map/psum | solution.py:19
  503.3 7.7 pmax.76
  511.5 6.2 psum.153
  518.0 67.4 %pmax.77 = f32[2048]{0:T(1024)S(1)} all-reduce(f32[2048]{0:T(1024)S(1)} %subtract_reduce_fusion.2), channel_id=1, replica_groups=mesh['row'=32,'col'=4] {'row'}, use_global_device_ids=true, to_apply=%region_31.0 | all-reduce | flops 2048 | bytes 16384 | tf_op jit(solution)/shard_map/pmax | solution.py:18
  586.2 63.7 %psum.154 = f32[2048]{0:T(1024)S(1)} all-reduce(f32[2048]{0:T(1024)S(1)} %exponential_reduce_fusion.2), channel_id=1, replica_groups=mesh['row'=32,'col'=4] {'row'}, use_global_device_ids=true, to_apply=%region_33.0 | all-reduce | flops 2048 | bytes 16384 | tf_op jit(solution)/shard_map/psum | solution.py:19
  650.2 7.7 pmax.78
  658.4 6.0 psum.155
  664.8 67.4 %pmax.79 = f32[2048]{0:T(1024)S(1)} all-reduce(f32[2048]{0:T(1024)S(1)} %subtract_reduce_fusion), channel_id=1, replica_groups=mesh['row'=32,'col'=4] {'row'}, use_global_device_ids=true, to_apply=%region_39.0 | all-reduce | flops 2048 | bytes 16384 | tf_op jit(solution)/shard_map/pmax | solution.py:18
  732.9 63.7 %psum.156 = f32[2048]{0:T(1024)S(1)} all-reduce(f32[2048]{0:T(1024)S(1)} %exponential_reduce_fusion), channel_id=1, replica_groups=mesh['row'=32,'col'=4] {'row'}, use_global_device_ids=true, to_apply=%region_41.0 | all-reduce | flops 2048 | bytes 16384 | tf_op jit(solution)/shard_map/psum | solution.py:19
  799.6 63.7 %psum.157 = f32[2048]{0:T(1024)S(1)} all-reduce(f32[2048]{0:T(1024)S(1)} %get-tuple-element.4), channel_id=1, replica_groups=mesh['row'=32,'col'=4] {'row'}, use_global_device_ids=true, to_apply=%region_43.0 | all-reduce | flops 2048 | bytes 16384 | tf_op jit(solution)/shard_map/psum | solution.py:67
  864.0 7.7 psum.158
  872.6 65.7 %psum.159 = f32[2048]{0:T(1024)S(1)} all-reduce(f32[2048]{0:T(1024)S(1)} %fusion.12), channel_id=1, replica_groups=mesh['row'=32,'col'=4] {'row'}, use_global_device_ids=true, to_apply=%region_48.0 | all-reduce | flops 2048 | bytes 16384 | tf_op jit(solution)/shard_map/psum | solution.py:85
  945.9 65.4 %psum.161 = f32[2048]{0:T(1024)S(1)} all-reduce(f32[2048]{0:T(1024)S(1)} %fusion.13), channel_id=1, replica_groups=mesh['row'=32,'col'=4] {'row'}, use_global_device_ids=true, to_apply=%region_52.0 | all-reduce | flops 2048 | bytes 16384 | tf_op jit(solution)/shard_map/psum | solution.py:85
  1012.0 7.7 psum.162
  1020.6 65.7 %psum.163 = f32[2048]{0:T(1024)S(1)} all-reduce(f32[2048]{0:T(1024)S(1)} %fusion.14), channel_id=1, replica_groups=mesh['row'=32,'col'=4] {'row'}, use_global_device_ids=true, to_apply=%region_56.0 | all-reduce | flops 2048 | bytes 16384 | tf_op jit(solution)/shard_map/psum | solution.py:85
  1093.9 65.4 %psum.165 = f32[2048]{0:T(1024)S(1)} all-reduce(f32[2048]{0:T(1024)S(1)} %fusion.15), channel_id=1, replica_groups=mesh['row'=32,'col'=4] {'row'}, use_global_device_ids=true, to_apply=%region_60.0 | all-reduce | flops 2048 | bytes 16384 | tf_op jit(solution)/shard_map/psum | solution.py:85
  1160.1 7.7 psum.166
  1167.8 8.2 fusion.25
  1181.3 11.4 reduce-scatter.2.cloned.1.call-done
  1192.7 89.7 %all-reduce.2.cloned.1.call-done = bf16[2048,64]{1,0:T(8,128)(2,1)} async-done(((bf16[2048,64]{1,0:T(8,128)(2,1)}), bf16[2048,64]{1,0:T(8,128)(2,1)}) %all-reduce.2.cloned.1.call-update) | async-done | bytes 262160 | tf_op jit(solution)/shard_map/psum | solution.py:99
  (75 shorter events, 46.2 us)
Async XLA Ops:
  8.0 1.1 copy-start
  8.0 1184.7 %reduce-scatter.2.cloned.1.call-start = ((), (), s32[]{:S(2)}) async-start(), calls=%async_computation.1 | async-start | bytes 81920 | tf_op jit(solution)/shard_map/reduce_scatter | solution.py:96
  61.5 16.2 %copy-start.3 = (f32[256]{0:T(256)S(1)}, f32[256]{0:T(256)}, u32[]{:S(2)}) copy-start(f32[256]{0:T(256)} %param.4) | copy-start | bytes 3076
  732.9 64.6 %copy-start.2 = (bf16[256,64]{0,1:T(8,128)(2,1)S(1)}, bf16[256,64]{0,1:T(8,128)(2,1)}, u32[]{:S(2)}) copy-start(bf16[256,64]{0,1:T(8,128)(2,1)} %param.3) | copy-start | bytes 98308
  1176.0 1.0 copy-start.1
  1178.1 104.3 %all-reduce.2.cloned.1.call-start = ((), (), s32[]{:S(2)}) async-start(), calls=%async_computation.2 | async-start | bytes 1048576 | tf_op jit(solution)/shard_map/psum | solution.py:99
Sparse Core Ops, SparseCore 0:
  1178.3 14.3 reduce-scatter.1
Sparse Core Ops, SparseCore 1:
  1181.8 100.5 all-reduce.1
where the time goes:
time: 1290 us
  blocking collectives  1140 us (88%)
  waiting for transfers between devices  101 us (8%)
  other arithmetic  26.4 us (2%)
  between operations  15.9 us (1%)
    pmax x5, blocking collectives, column_lse(): highest = lax.pmax(jnp.max(logits, axis=0), 'row')  337 us
    psum x5, blocking collectives, column_lse(): lax.psum(jnp.sum(jnp.exp(logits - highest[None, :]), axis=0), 'row')  318 us
    psum x4, blocking collectives, local(): col_grad = -lax.psum(jnp.sum(back_tile * row_grad[:, None], axis=0), 'row')  262 us
    psum x1, waiting for transfers between devices, local(): summed = lax.psum(col_term.astype(jnp.bfloat16), 'row').astype(jnp.float32)  89.7 us
    psum x1, blocking collectives, local(): col_grad = lax.psum(jnp.sum(weighted, axis=0), 'row')  63.7 us
    pmax x5, blocking collectives, row_lse(): highest = lax.pmax(jnp.max(logits, axis=1), 'col')  39.4 us
    psum x5, blocking collectives, local(): lax.psum(surplus - jnp.sum(column_soft * col_grad[None, :], axis=1), 'col')  35.2 us
    psum x5, blocking collectives, row_lse(): lax.psum(jnp.sum(jnp.exp(logits - highest[:, None]), axis=1), 'col')  30.3 us
  transfers between devices with their start and end apart: 2, of which 2 were waited for; matrix products, arithmetic and copies ran while one was open for 0% of the time, Pallas kernels for 0%

commit v1 on v0

v1 whole, which is shorter than its diff:
```python
import math

import jax
import jax.numpy as jnp
from jax import lax
from jax.sharding import PartitionSpec as P

ITERS = 5
BOTH = ("row", "col")
X0, CORE, Y0, Z0 = 1, 4, 8, 32
LW_TOP = 145.0
TINY = 1e-37


def swap(value, bit, only=None, one_way=False):
    pairs = [(i, i ^ bit) for i in range(128) if only is None or i & only]
    return lax.ppermute(value, BOTH, pairs)


def merge(a, b):
    top = jnp.maximum(a, b)
    return top + jnp.log(jnp.exp(a - top) + jnp.exp(b - top))


def plus(a, b):
    return a + b


def over_rows(partial, op, core):
    both = op(partial, swap(partial, CORE))
    got = op(both, swap(both, Y0, CORE))
    got = op(got, swap(got, Z0, CORE))
    back = swap(got, CORE, CORE)
    return jnp.where(core == 1, got, back)


def over_cols(partial, op):
    return op(partial, swap(partial, X0))


def split3(v):
    hi = lax.reduce_precision(v, 8, 7)
    rest = v - hi
    mid = lax.reduce_precision(rest, 8, 7)
    return tuple(part.astype(jnp.bfloat16) for part in (hi, mid, rest - mid))


def dot_t(a, b):
    return lax.dot_general(a, b, (((1,), (1,)), ((), ())), preferred_element_type=jnp.float32)


def local(positions, log_weights, cotangent):
    row = lax.axis_index("row")
    col = lax.axis_index("col")
    x0, x1 = col % 2, col // 2
    core, y0, y1 = row % 2, (row // 2) % 2, (row // 4) % 2
    z0, z1 = (row // 8) % 2, row // 16
    n_row, dim = positions.shape
    piece = n_row // 4
    half = n_row // 2
    total = n_row * 32
    log_count = math.log(total)
    scale = 4.0 / dim

    def take(v):
        v = v.reshape((2, 2, piece) + v.shape[1:])
        return lax.dynamic_index_in_dim(v, x0, 1, keepdims=False).reshape((half,) + v.shape[3:])

    wide = jnp.concatenate([take(positions), take(cotangent)], axis=1)
    lw3 = jnp.stack(split3(take(log_weights)) + (jnp.zeros((half,), jnp.bfloat16),) * 13)
    payload = jnp.concatenate([wide, lw3], axis=0)
    full = lax.all_to_all(
        jnp.broadcast_to(payload[None], (32,) + payload.shape), "row", 0, 0, tiled=True
    )
    n_col = 32 * half
    col_pos = full[:, :half, :dim].reshape(n_col, dim)
    col_cot = full[:, :half, dim:].reshape(n_col, dim)
    near = full.reshape((2, 2, 2, 2, 2) + payload.shape)
    near = lax.dynamic_index_in_dim(near, core, 4, keepdims=False)
    near = lax.dynamic_index_in_dim(near, y0, 3, keepdims=False)
    near = lax.dynamic_index_in_dim(near, z0, 1, keepdims=False).reshape((4,) + payload.shape)
    far = swap(near, X0)
    first = jnp.where(x0 == 0, near, far)
    second = jnp.where(x0 == 0, far, near)
    both = jnp.stack([first, second], axis=1)
    row_pos = both[:, :, :half, :dim].reshape(4, 2, 2, piece, dim)
    row_pos = row_pos.transpose(0, 2, 1, 3, 4).reshape(4 * n_row, dim)
    lwr = both[:, :, half : half + 3, :].astype(jnp.float32)
    lwr = (lwr[:, :, 0] + lwr[:, :, 1]) + lwr[:, :, 2]
    lw = lwr.reshape(4, 2, 2, piece).transpose(0, 2, 1, 3).reshape(4 * n_row)

    row_f32 = row_pos.astype(jnp.float32)
    col_f32 = col_pos.astype(jnp.float32)
    row_sq = scale * jnp.sum(row_f32 * row_f32, axis=1)
    col_sq = scale * jnp.sum(col_f32 * col_f32, axis=1)

    def logits(row_vec, col_vec):
        cross = dot_t(row_pos, col_pos)
        return (2.0 * scale) * cross + row_vec[:, None] + col_vec[None, :]

    neg = logits(-row_sq, -col_sq)
    top = jnp.max(neg, axis=1)
    mass = jnp.sum(jnp.exp(logits(-row_sq - top, -col_sq)), axis=1)
    row_lse = over_cols(top + jnp.log(mass), merge)
    u = log_count - row_lse
    us, vs = [u], [jnp.zeros((n_col,), jnp.float32)]
    shift = jnp.full((n_col,), LW_TOP + log_count, jnp.float32)
    for k in range(ITERS):
        mass = jnp.sum(jnp.exp(logits(us[k] + lw - row_sq, -col_sq - shift)), axis=0)
        v = -over_rows(shift + jnp.log(jnp.maximum(mass, TINY)), merge, core)
        vs.append(v)
        if k == ITERS - 1:
            break
        shift = (log_count - us[k]) + jnp.max(v - vs[k])
        mass = jnp.sum(jnp.exp(logits(-row_sq - shift, v - col_sq)), axis=1)
        u = log_count - over_cols(shift + jnp.log(jnp.maximum(mass, TINY)), merge)
        us.append(u)
        shift = -v + jnp.max(u - us[k])

    def soft(k):
        return jnp.exp(logits(us[k] + lw - row_sq, vs[k + 1] - col_sq))

    def back(k):
        return jnp.exp(logits(us[k] - log_count - row_sq, vs[k] - col_sq))

    dus, dvs = [None] * ITERS, [None] * ITERS
    last = ITERS - 1
    dvs[last] = over_rows(jnp.sum(soft(last) * dot_t(row_pos, col_cot), axis=0), plus, core)
    dus[last] = over_cols(
        jnp.sum(soft(last) * (dot_t(row_pos, col_cot) - dvs[last][None, :]), axis=1), plus
    )
    for k in reversed(range(last)):
        dvs[k] = -over_rows(jnp.sum(back(k + 1) * dus[k + 1][:, None], axis=0), plus, core)
        dus[k] = -over_cols(jnp.sum(soft(k) * dvs[k][None, :], axis=1), plus)

    at = (z1 * 2 + y1) * n_row

    def rows(v):
        return lax.dynamic_slice_in_dim(v, at, n_row, -1)

    def cols(v):
        v = v.reshape(v.shape[:-1] + (32, 2, piece))
        v = lax.dynamic_index_in_dim(v, x1, v.ndim - 2, keepdims=False)
        return v.reshape(v.shape[:-2] + (32 * piece,))

    u_t = rows(jnp.stack(us))
    du_t = rows(jnp.stack(dus))
    v_t = cols(jnp.stack(vs))
    dv_t = cols(jnp.stack(dvs))
    both_t = lax.dynamic_index_in_dim(
        full[:, :half].reshape(32, 2, piece, 2 * dim), x1, 1, keepdims=False
    ).reshape(32 * piece, 2 * dim)
    pos_t, cot_t = both_t[:, :dim], both_t[:, dim:]
    own_f32 = positions.astype(jnp.float32)
    pos_t32 = pos_t.astype(jnp.float32)
    own_sq = scale * jnp.sum(own_f32 * own_f32, axis=1)
    pos_sq = scale * jnp.sum(pos_t32 * pos_t32, axis=1)
    base = (2.0 * scale) * dot_t(positions, pos_t) - own_sq[:, None] - pos_sq[None, :]
    paired = dot_t(positions, cot_t)
    plan = None
    grad = None
    for k in reversed(range(ITERS)):
        s = jnp.exp(base + (u_t[k] + log_weights)[:, None] + v_t[k + 1][None, :])
        if plan is None:
            plan = s
            grad = s * (dv_t[k][None, :] - paired)
        else:
            grad = grad + s * dv_t[k][None, :]
        r = jnp.exp(base + (u_t[k] - log_count)[:, None] + v_t[k][None, :])
        grad = grad + r * du_t[k][:, None]
    row_mass = jnp.sum(grad, axis=1)
    col_mass = jnp.sum(grad, axis=0)
    narrow = grad.astype(jnp.bfloat16)
    direct = jnp.dot(plan.astype(jnp.bfloat16), cot_t, preferred_element_type=jnp.float32)
    pulled = jnp.dot(narrow, pos_t, preferred_element_type=jnp.float32)
    pushed = lax.dot_general(
        narrow, positions, (((0,), (0,)), ((), ())), preferred_element_type=jnp.float32
    )
    row_term = direct + 2.0 * scale * (row_mass[:, None] * own_f32 - pulled)
    col_term = 2.0 * scale * (col_mass[:, None] * pos_t32 - pushed)
    row_parts = lax.all_to_all(
        row_term.astype(jnp.bfloat16).reshape(4, piece, dim), "col", 0, 0, tiled=True
    )
    col_parts = lax.all_to_all(
        col_term.astype(jnp.bfloat16).reshape(32, piece, dim), "row", 0, 0, tiled=True
    )
    out = jnp.sum(row_parts.astype(jnp.float32), axis=0) + jnp.sum(
        col_parts.astype(jnp.float32), axis=0
    )
    grad_log_weights = ((((du_t[4] + du_t[3]) + du_t[2]) + du_t[1]) + du_t[0])
    return (out, grad_log_weights)


def solution(mesh):
    in_specs = (P("row", None), P("row"), P("row", None))
    out_specs = (P(("row", "col"), None), P("row"))
    return jax.shard_map(local, mesh=mesh, in_specs=in_specs, out_specs=out_specs, check_vma=False)
```

time: 1290 us -> 433 us (0.34)
  blocking collectives: 1140 us -> 0 us
  other arithmetic: 26.4 us -> 168 us
  starting transfers between devices: 0.08 us -> 104 us
  matrix products: 7.84 us -> 31.3 us
  local copies, waits for them, and re-layouts: 2.06 us -> 18 us
  between operations: 15.9 us -> 2.26 us
    psum x20 -> x0, blocking collectives: 710 us -> none  [the longest x5 318 us: column_lse(): lax.psum(jnp.sum(jnp.exp(logits - highest[None, :]), axis=0), 'row')]
    pmax x10 -> x0, blocking collectives: 376 us -> none  [the longest x5 337 us: column_lse(): highest = lax.pmax(jnp.max(logits, axis=0), 'row')]
    reduce_sum x22 -> x25, other arithmetic: 21.1 us -> 152 us  [the longest x5 46.4 us: local(): jnp.sum(jnp.exp(logits(us[k] + lw - row_sq, -col_sq - shift)), axis=0)]
    psum x1 -> x0, waiting for transfers between devices: 89.7 us -> none  [local(): summed = lax.psum(col_term.astype(jnp.bfloat16), 'row').astype(jnp.float32)]
    ppermute x0 -> x51, starting transfers between devices: none -> 85.3 us  [swap(): return lax.ppermute(value, BOTH, pairs)]
    ppermute x0 -> x51, waiting for transfers between devices: none -> 73.3 us  [swap(): return lax.ppermute(value, BOTH, pairs)]
    all_gather x2 -> x0, blocking collectives: 51.9 us -> none  [the longest x1 27.6 us: local(): lax.all_gather(own_pos, 'row', axis=0, tiled=True)]
    all_to_all x0 -> x3, waiting for transfers between devices: none -> 27.5 us  [the longest x1 18.4 us: local(): lax.all_to_all(jnp.broadcast_to(payload[None], (32,) + payload.shape), 'r...]
  transfers between devices with their start and end apart: 2 -> 54, of which waited for: 2 -> 53; matrix products, arithmetic and copies ran while one was open for 0% -> 3% of each run, Pallas kernels for 0% -> 0%
where the time goes in v1:
time: 433 us; the launch traced here: 425 us
  other arithmetic  168 us (39%)
  starting transfers between devices  104 us (24%)
  waiting for transfers between devices  101 us (23%)
  matrix products  31.3 us (7%)
  local copies, waits for them, and re-layouts  18 us (4%)
    ppermute x51, starting transfers between devices, swap(): return lax.ppermute(value, BOTH, pairs)  85.3 us
    ppermute x51, waiting for transfers between devices, swap(): return lax.ppermute(value, BOTH, pairs)  73.3 us
    reduce_sum x5, other arithmetic, local(): jnp.sum(jnp.exp(logits(us[k] + lw - row_sq, -col_sq - shift)), axis=0)  46.4 us
    reduce_sum x4, other arithmetic, local(): mass = jnp.sum(jnp.exp(logits(-row_sq - shift, v - col_sq)), axis=1)  34.6 us
    dot_general x4, matrix products, dot_t(): lax.dot_general(a, b, (((1,), (1,)), ((), ())), preferred_element_type=jn...  28.3 us
    reduce_sum x4, other arithmetic, local(): dus[k] = -over_cols(jnp.sum(soft(k) * dvs[k][None, :], axis=1), plus)  27.8 us
    reduce_sum x4, other arithmetic, local(): jnp.sum(back(k + 1) * dus[k + 1][:, None], axis=0)  24.5 us
    all_to_all x1, waiting for transfers between devices, local(): lax.all_to_all(jnp.broadcast_to(payload[None], (32,) + payload.shape), 'r...  18.4 us
  transfers between devices with their start and end apart: 54, of which 53 were waited for; matrix products, arithmetic and copies ran while one was open for 3% of the time, Pallas kernels for 0%

profile of v1, /device:TPU:1, one launch (start us, length us, event | category | flops | bytes accessed | tf_op | source)
XLA Modules:
  0.0 424.7 jit_solution(4433814016074354174)
XLA Ops:
  5.8 9.6 %all-to-all-start = ((bf16[32,144,128]{2,1,0:T(8,128)(2,1)}), bf16[32,144,128]{2,1,0:T(8,128)(2,1)S(1)}, u32[]{:S(2)}, u32[]{:S(2)}) async-start(bf16[32,144,128]{2,1,0:T(8,128)(2,1)} %broadcast_in_dim.4), calls=%async_computation | async-start | bytes 2359296 | tf_op jit(solution)/shard_map/all_to_all | solution.py:72
  15.5 18.4 %all-to-all-done = bf16[32,144,128]{2,1,0:T(8,128)(2,1)S(1)} async-done(((bf16[32,144,128]{2,1,0:T(8,128)(2,1)}), bf16[32,144,128]{2,1,0:T(8,128)(2,1)S(1)}, u32[]{:S(2)}, u32[]{:S(2)}) %all-to-all-start) | async-done | bytes 1179680 | tf_op jit(solution)/shard_map/all_to_all | solution.py:72
  41.8 7.5 %add_reduce_fusion = (f32[1024]{0:T(1024)S(1)}, f32[1024,4096]{1,0:T(8,128)}) fusion(f32[4096]{0:T(1024)S(1)} %get-tuple-element.60, f32[1024]{0:T(1024)S(1)} %neg.74, bf16[1024,64]{0,1:T(8,128)(2,1)S(1)} %reshape.282, bf16[4096,64]{1,0:T(8,128)(2,1)S(1)} %bitcast.107), kind=kOutput, calls=%fused_computation.21 | convolution fusion | flops 553647104 | bytes 17457152 | tf_op jit(solution)/shard_map/dot_general | solution.py:49
  49.4 8.6 %exponential_reduce_fusion.9 = f32[1024]{0:T(1024)S(1)} fusion(f32[1024,4096]{1,0:T(8,128)} %get-tuple-element.80, f32[1024]{0:T(1024)S(1)} %negate_subtract_fusion, f32[4096]{0:T(1024)S(1)} %get-tuple-element.60), kind=kLoop, calls=%fused_computation.20 | loop fusion | flops 12581888 | bytes 16801792 | tf_op jit(solution)/shard_map/reduce_sum | solution.py:103
  60.8 9.3 %exponential_reduce_fusion.8 = f32[4096]{0:T(1024)S(1)} fusion(f32[1024,4096]{1,0:T(8,128)} %get-tuple-element.80, f32[4096]{0:T(1024)S(1)} %get-tuple-element.61, f32[1024]{0:T(1024)S(1)} %get-tuple-element.39), kind=kLoop, calls=%fused_computation.19 | loop fusion | flops 12578816 | bytes 16814080 | tf_op jit(solution)/shard_map/reduce_sum | solution.py:109
  79.9 2.6 collective-permute-done.4
  85.8 8.6 %exponential_reduce_fusion.7 = f32[1024]{0:T(1024)S(1)} fusion(f32[1024,4096]{1,0:T(8,128)} %get-tuple-element.80, f32[4096]{0:T(1024)S(1)} %bitcast_subtract_fusion.4, f32[1024]{0:T(1024)S(1)} %fusion.49), kind=kLoop, calls=%fused_computation.18 | loop fusion | flops 12581888 | bytes 16801792 | tf_op jit(solution)/shard_map/reduce_sum | solution.py:115
  99.0 9.2 %exponential_reduce_fusion.6 = f32[4096]{0:T(1024)S(1)} fusion(f32[1024,4096]{1,0:T(8,128)} %get-tuple-element.80, f32[4096]{0:T(1024)S(1)} %add_subtract_fusion.3, f32[1024]{0:T(1024)S(1)} %get-tuple-element.35), kind=kLoop, calls=%fused_computation.17 | loop fusion | flops 12578816 | bytes 16814080 | tf_op jit(solution)/shard_map/reduce_sum | solution.py:109
  117.8 2.6 collective-permute-done.9
  123.7 8.6 %exponential_reduce_fusion.5 = f32[1024]{0:T(1024)S(1)} fusion(f32[1024,4096]{1,0:T(8,128)} %get-tuple-element.80, f32[4096]{0:T(1024)S(1)} %bitcast_subtract_fusion.3, f32[1024]{0:T(1024)S(1)} %fusion.50), kind=kLoop, calls=%fused_computation.16 | loop fusion | flops 12581888 | bytes 16801792 | tf_op jit(solution)/shard_map/reduce_sum | solution.py:115
  136.9 9.2 %exponential_reduce_fusion.4 = f32[4096]{0:T(1024)S(1)} fusion(f32[1024,4096]{1,0:T(8,128)} %get-tuple-element.80, f32[4096]{0:T(1024)S(1)} %add_subtract_fusion.2, f32[1024]{0:T(1024)S(1)} %get-tuple-element.31), kind=kLoop, calls=%fused_computation.15 | loop fusion | flops 12578816 | bytes 16814080 | tf_op jit(solution)/shard_map/reduce_sum | solution.py:109
  155.6 2.6 collective-permute-done.14
  161.6 8.6 %exponential_reduce_fusion.3 = f32[1024]{0:T(1024)S(1)} fusion(f32[1024,4096]{1,0:T(8,128)} %get-tuple-element.80, f32[4096]{0:T(1024)S(1)} %bitcast_subtract_fusion.2, f32[1024]{0:T(1024)S(1)} %fusion.51), kind=kLoop, calls=%fused_computation.14 | loop fusion | flops 12581888 | bytes 16801792 | tf_op jit(solution)/shard_map/reduce_sum | solution.py:115
  174.9 9.2 %exponential_reduce_fusion.2 = f32[4096]{0:T(1024)S(1)} fusion(f32[1024,4096]{1,0:T(8,128)} %get-tuple-element.80, f32[4096]{0:T(1024)S(1)} %add_subtract_fusion.1, f32[1024]{0:T(1024)S(1)} %get-tuple-element.27), kind=kLoop, calls=%fused_computation.13 | loop fusion | flops 12578816 | bytes 16814080 | tf_op jit(solution)/shard_map/reduce_sum | solution.py:109
  193.7 2.6 collective-permute-done.19
  199.7 8.6 %exponential_reduce_fusion.1 = f32[1024]{0:T(1024)S(1)} fusion(f32[1024,4096]{1,0:T(8,128)} %get-tuple-element.80, f32[4096]{0:T(1024)S(1)} %bitcast_subtract_fusion.1, f32[1024]{0:T(1024)S(1)} %fusion.52), kind=kLoop, calls=%fused_computation.12 | loop fusion | flops 12581888 | bytes 16801792 | tf_op jit(solution)/shard_map/reduce_sum | solution.py:115
  212.8 9.4 %exponential_reduce_fusion = f32[4096]{0:T(1024)S(1)} fusion(f32[1024,4096]{1,0:T(8,128)} %get-tuple-element.80, f32[4096]{0:T(1024)S(1)} %add_subtract_fusion, f32[1024]{0:T(1024)S(1)} %get-tuple-element.23), kind=kLoop, calls=%fused_computation.11 | loop fusion | flops 12578816 | bytes 16814080 | tf_op jit(solution)/shard_map/reduce_sum | solution.py:109
  231.7 2.6 collective-permute-done.24
  236.5 14.2 %multiply_reduce_fusion.9 = (f32[4096]{0:T(1024)S(1)}, f32[1024,4096]{1,0:T(8,128)}) fusion(f32[1024,4096]{1,0:T(8,128)} %get-tuple-element.80, f32[4096]{0:T(1024)S(1)} %get-tuple-element.21, f32[1024]{0:T(1024)S(1)} %get-tuple-element.23, bf16[1024,64]{0,1:T(8,128)(2,1)S(1)} %reshape.282, bf16[4096,64]{1,0:T(8,128)(2,1)} %bitcast.106), kind=kOutput, calls=%fused_computation.9 | convolution fusion | flops 553644032 | bytes 34246656 | tf_op jit(solution)/shard_map/dot_general | solution.py:49
  263.0 8.5 %multiply_reduce_fusion.8 = f32[1024]{0:T(1024)S(1)} fusion(f32[1024,4096]{1,0:T(8,128)} %get-tuple-element.82, f32[1024,4096]{1,0:T(8,128)S(1)} %bitcast.99, f32[4096]{0:T(1024)S(1)} %broadcast_select_fusion, f32[4096]{0:T(1024)S(1)} %get-tuple-element.21, f32[1024]{0:T(1024)S(1)} %get-tuple-element.23), kind=kLoop, calls=%fused_computation.8 | loop fusion | flops 20970496 | bytes 33595392 | tf_op jit(solution)/shard_map/reduce_sum | solution.py:130
  274.0 4.4 %multiply_reduce_fusion.7 = f32[4096]{0:T(1024)S(1)} fusion(f32[1024,4096]{1,0:T(8,128)S(1)} %bitcast.99, f32[1024]{0:T(1024)S(1)} %add.1094, f32[1024]{0:T(1024)S(1)} %get-tuple-element.65, f32[4096]{0:T(1024)S(1)} %bitcast_subtract_fusion.1), kind=kLoop, calls=%fused_computation.7 | loop fusion | flops 16773120 | bytes 16818176 | tf_op jit(solution)/shard_map/reduce_sum | solution.py:133
  291.9 4.1 multiply_reduce_fusion.6
  298.6 4.4 %multiply_reduce_fusion.5 = f32[4096]{0:T(1024)S(1)} fusion(f32[1024,4096]{1,0:T(8,128)S(1)} %bitcast.99, f32[1024]{0:T(1024)S(1)} %add_negate_fusion.3, f32[1024]{0:T(1024)S(1)} %get-tuple-element.64, f32[4096]{0:T(1024)S(1)} %bitcast_subtract_fusion.2), kind=kLoop, calls=%fused_computation.5 | loop fusion | flops 16773120 | bytes 16818176 | tf_op jit(solution)/shard_map/reduce_sum | solution.py:133
  316.4 7.9 %multiply_reduce_fusion.4 = f32[1024]{0:T(1024)S(1)} fusion(f32[1024,4096]{1,0:T(8,128)} %get-tuple-element.80, f32[4096]{0:T(1024)S(1)} %select_negate_fusion.2, f32[4096]{0:T(1024)S(1)} %bitcast_subtract_fusion.2, f32[1024]{0:T(1024)S(1)} %get-tuple-element.31), kind=kLoop, calls=%fused_computation.4 | loop fusion | flops 16776192 | bytes 16818176 | tf_op jit(solution)/shard_map/reduce_sum | solution.py:134
  326.9 7.9 %multiply_reduce_fusion.3 = f32[4096]{0:T(1024)S(1)} fusion(f32[1024,4096]{1,0:T(8,128)} %get-tuple-element.80, f32[1024]{0:T(1024)S(1)} %add_negate_fusion.2, f32[1024]{0:T(1024)S(1)} %get-tuple-element.63, f32[4096]{0:T(1024)S(1)} %bitcast_subtract_fusion.3), kind=kLoop, calls=%fused_computation.3 | loop fusion | flops 16773120 | bytes 16818176 | tf_op jit(solution)/shard_map/reduce_sum | solution.py:133
  348.5 7.9 %multiply_reduce_fusion.2 = f32[1024]{0:T(1024)S(1)} fusion(f32[1024,4096]{1,0:T(8,128)} %get-tuple-element.80, f32[4096]{0:T(1024)S(1)} %select_negate_fusion.1, f32[4096]{0:T(1024)S(1)} %bitcast_subtract_fusion.3, f32[1024]{0:T(1024)S(1)} %get-tuple-element.35), kind=kLoop, calls=%fused_computation.2 | loop fusion | flops 16776192 | bytes 16818176 | tf_op jit(solution)/shard_map/reduce_sum | solution.py:134
  359.0 7.9 %multiply_reduce_fusion.1 = f32[4096]{0:T(1024)S(1)} fusion(f32[1024,4096]{1,0:T(8,128)} %get-tuple-element.80, f32[1024]{0:T(1024)S(1)} %add_negate_fusion.1, f32[1024]{0:T(1024)S(1)} %get-tuple-element.62, f32[4096]{0:T(1024)S(1)} %bitcast_subtract_fusion.4), kind=kLoop, calls=%fused_computation.1 | loop fusion | flops 16773120 | bytes 16818176 | tf_op jit(solution)/shard_map/reduce_sum | solution.py:133
  381.3 7.9 %multiply_reduce_fusion = f32[1024]{0:T(1024)S(1)} fusion(f32[1024,4096]{1,0:T(8,128)} %get-tuple-element.80, f32[4096]{0:T(1024)S(1)} %select_negate_fusion, f32[4096]{0:T(1024)S(1)} %bitcast_subtract_fusion.4, f32[1024]{0:T(1024)S(1)} %get-tuple-element.39), kind=kLoop, calls=%fused_computation | loop fusion | flops 16776192 | bytes 16818176 | tf_op jit(solution)/shard_map/reduce_sum | solution.py:134
  392.1 6.1 %fusion.57 = (f32[2048]{0:T(1024)S(1)}, f32[256]{0:T(256)S(1)}, bf16[2048,256]{1,0:T(8,128)(2,1)S(1)}) fusion(f32[256]{0:T(256)S(1)} %bitcast.139, f32[2048]{0:T(1024)S(1)} %add.1167, f32[2048,256]{1,0:T(8,128)S(1)} %fusion.6, f32[256]{0:T(256)S(1)} %get-tuple-element.75, f32[2048]{0:T(1024)S(1)} %mul.352, f32[256]{0:T(256)S(1)} %get-tuple-element.74, ...), kind=kOutput, calls=%fused_computation.243 | convolution fusion | flops 89650944 | bytes 3817472 | tf_op jit(solution)/shard_map/dot_general | solution.py:49
  400.4 4.0 all-to-all-start.1
  408.8 5.3 %all-to-all-start.2 = ((bf16[32,2,2048]{2,1,0:T(2,128)(2,1)}), bf16[32,2,2048]{2,1,0:T(2,128)(2,1)S(1)}, u32[]{:S(2)}, u32[]{:S(2)}) async-start(bf16[32,2,2048]{2,1,0:T(2,128)(2,1)} %reshape.355), calls=%async_computation.2 | async-start | bytes 524288 | tf_op jit(solution)/shard_map/all_to_all | solution.py:184
  414.8 8.3 %all-to-all-done.2 = bf16[32,2,2048]{2,1,0:T(2,128)(2,1)S(1)} async-done(((bf16[32,2,2048]{2,1,0:T(2,128)(2,1)}), bf16[32,2,2048]{2,1,0:T(2,128)(2,1)S(1)}, u32[]{:S(2)}, u32[]{:S(2)}) %all-to-all-start.2) | async-done | bytes 262176 | tf_op jit(solution)/shard_map/all_to_all | solution.py:184
  (293 shorter events, 185.7 us)
Async XLA Ops:
  5.8 28.1 %all-to-all-start = ((bf16[32,144,128]{2,1,0:T(8,128)(2,1)}), bf16[32,144,128]{2,1,0:T(8,128)(2,1)S(1)}, u32[]{:S(2)}, u32[]{:S(2)}) async-start(bf16[32,144,128]{2,1,0:T(8,128)(2,1)} %broadcast_in_dim.4), calls=%async_computation | async-start | bytes 2359296 | tf_op jit(solution)/shard_map/all_to_all | solution.py:72
  34.0 5.1 %collective-permute-start = (bf16[4,144,128]{2,1,0:T(8,128)(2,1)S(1)}, bf16[4,144,128]{2,1,0:T(8,128)(2,1)S(1)}, u32[]{:S(2)}, u32[]{:S(2)}) collective-permute-start(bf16[4,144,128]{2,1,0:T(8,128)(2,1)S(1)} %bitcast.113), channel_id=1, source_target_pairs={{0,1},{1,0},{2,3},{3,2},{4,5},{5,4},{6,7},{7,6},{8,9},{9,8},{10,11... | collective-permute-start | bytes 442376 | tf_op jit(solution)/shard_map/ppermute | solution.py:17
  58.1 2.7 collective-permute-start.1
  70.1 3.3 collective-permute-start.2
  73.4 4.5 %collective-permute-start.3 = (f32[4096]{0:T(1024)S(1)}, f32[4096]{0:T(1024)S(1)}, u32[]{:S(2)}, u32[]{:S(2)}) collective-permute-start(f32[4096]{0:T(1024)S(1)} %log_add_fusion.18), channel_id=1, source_target_pairs={{4,12},{5,13},{6,14},{7,15},{12,4},{13,5},{14,6},{15,7},{20,28},{2... | collective-permute-start | bytes 49160 | tf_op jit(solution)/shard_map/ppermute | solution.py:17
  78.0 4.5 %collective-permute-start.4 = (f32[4096]{0:T(1024)S(1)}, f32[4096]{0:T(1024)S(1)}, u32[]{:S(2)}, u32[]{:S(2)}) collective-permute-start(f32[4096]{0:T(1024)S(1)} %log_add_fusion.17), channel_id=1, source_target_pairs={{4,36},{5,37},{6,38},{7,39},{12,44},{13,45},{14,46},{15,47},{20,52... | collective-permute-start | bytes 49160 | tf_op jit(solution)/shard_map/ppermute | solution.py:17
  111.3 4.5 %collective-permute-start.8 = (f32[4096]{0:T(1024)S(1)}, f32[4096]{0:T(1024)S(1)}, u32[]{:S(2)}, u32[]{:S(2)}) collective-permute-start(f32[4096]{0:T(1024)S(1)} %log_add_fusion.14), channel_id=1, source_target_pairs={{4,12},{5,13},{6,14},{7,15},{12,4},{13,5},{14,6},{15,7},{20,28},{2... | collective-permute-start | bytes 49160 | tf_op jit(solution)/shard_map/ppermute | solution.py:17
  115.8 4.5 %collective-permute-start.9 = (f32[4096]{0:T(1024)S(1)}, f32[4096]{0:T(1024)S(1)}, u32[]{:S(2)}, u32[]{:S(2)}) collective-permute-start(f32[4096]{0:T(1024)S(1)} %log_add_fusion.13), channel_id=1, source_target_pairs={{4,36},{5,37},{6,38},{7,39},{12,44},{13,45},{14,46},{15,47},{20,52... | collective-permute-start | bytes 49160 | tf_op jit(solution)/shard_map/ppermute | solution.py:17
  133.0 2.5 collective-permute-start.11
  149.2 4.5 %collective-permute-start.13 = (f32[4096]{0:T(1024)S(1)}, f32[4096]{0:T(1024)S(1)}, u32[]{:S(2)}, u32[]{:S(2)}) collective-permute-start(f32[4096]{0:T(1024)S(1)} %log_add_fusion.10), channel_id=1, source_target_pairs={{4,12},{5,13},{6,14},{7,15},{12,4},{13,5},{14,6},{15,7},{20,28},{2... | collective-permute-start | bytes 49160 | tf_op jit(solution)/shard_map/ppermute | solution.py:17
  153.7 4.5 %collective-permute-start.14 = (f32[4096]{0:T(1024)S(1)}, f32[4096]{0:T(1024)S(1)}, u32[]{:S(2)}, u32[]{:S(2)}) collective-permute-start(f32[4096]{0:T(1024)S(1)} %log_add_fusion.9), channel_id=1, source_target_pairs={{4,36},{5,37},{6,38},{7,39},{12,44},{13,45},{14,46},{15,47},{20,52... | collective-permute-start | bytes 49160 | tf_op jit(solution)/shard_map/ppermute | solution.py:17
  170.9 2.7 collective-permute-start.16
  187.2 4.5 %collective-permute-start.18 = (f32[4096]{0:T(1024)S(1)}, f32[4096]{0:T(1024)S(1)}, u32[]{:S(2)}, u32[]{:S(2)}) collective-permute-start(f32[4096]{0:T(1024)S(1)} %log_add_fusion.6), channel_id=1, source_target_pairs={{4,12},{5,13},{6,14},{7,15},{12,4},{13,5},{14,6},{15,7},{20,28},{2... | collective-permute-start | bytes 49160 | tf_op jit(solution)/shard_map/ppermute | solution.py:17
  191.8 4.5 %collective-permute-start.19 = (f32[4096]{0:T(1024)S(1)}, f32[4096]{0:T(1024)S(1)}, u32[]{:S(2)}, u32[]{:S(2)}) collective-permute-start(f32[4096]{0:T(1024)S(1)} %log_add_fusion.5), channel_id=1, source_target_pairs={{4,36},{5,37},{6,38},{7,39},{12,44},{13,45},{14,46},{15,47},{20,52... | collective-permute-start | bytes 49160 | tf_op jit(solution)/shard_map/ppermute | solution.py:17
  209.0 2.5 collective-permute-start.21
  225.3 4.5 %collective-permute-start.23 = (f32[4096]{0:T(1024)S(1)}, f32[4096]{0:T(1024)S(1)}, u32[]{:S(2)}, u32[]{:S(2)}) collective-permute-start(f32[4096]{0:T(1024)S(1)} %log_add_fusion.2), channel_id=1, source_target_pairs={{4,12},{5,13},{6,14},{7,15},{12,4},{13,5},{14,6},{15,7},{20,28},{2... | collective-permute-start | bytes 49160 | tf_op jit(solution)/shard_map/ppermute | solution.py:17
  229.8 4.5 %collective-permute-start.24 = (f32[4096]{0:T(1024)S(1)}, f32[4096]{0:T(1024)S(1)}, u32[]{:S(2)}, u32[]{:S(2)}) collective-permute-start(f32[4096]{0:T(1024)S(1)} %log_add_fusion.1), channel_id=1, source_target_pairs={{4,36},{5,37},{6,38},{7,39},{12,44},{13,45},{14,46},{15,47},{20,52... | collective-permute-start | bytes 49160 | tf_op jit(solution)/shard_map/ppermute | solution.py:17
  251.9 4.5 %collective-permute-start.27 = (f32[4096]{0:T(1024)S(1)}, f32[4096]{0:T(1024)S(1)}, u32[]{:S(2)}, u32[]{:S(2)}) collective-permute-start(f32[4096]{0:T(1024)S(1)} %add.1091), channel_id=1, source_target_pairs={{4,12},{5,13},{6,14},{7,15},{12,4},{13,5},{14,6},{15,7},{20,28},{2... | collective-permute-start | bytes 49160 | tf_op jit(solution)/shard_map/ppermute | solution.py:17
  256.4 4.5 %collective-permute-start.28 = (f32[4096]{0:T(1024)S(1)}, f32[4096]{0:T(1024)S(1)}, u32[]{:S(2)}, u32[]{:S(2)}) collective-permute-start(f32[4096]{0:T(1024)S(1)} %add.1092), channel_id=1, source_target_pairs={{4,36},{5,37},{6,38},{7,39},{12,44},{13,45},{14,46},{15,47},{20,52... | collective-permute-start | bytes 49160 | tf_op jit(solution)/shard_map/ppermute | solution.py:17
  280.8 4.5 %collective-permute-start.32 = (f32[4096]{0:T(1024)S(1)}, f32[4096]{0:T(1024)S(1)}, u32[]{:S(2)}, u32[]{:S(2)}) collective-permute-start(f32[4096]{0:T(1024)S(1)} %add.1095), channel_id=1, source_target_pairs={{4,12},{5,13},{6,14},{7,15},{12,4},{13,5},{14,6},{15,7},{20,28},{2... | collective-permute-start | bytes 49160 | tf_op jit(solution)/shard_map/ppermute | solution.py:17
  285.3 4.5 %collective-permute-start.33 = (f32[4096]{0:T(1024)S(1)}, f32[4096]{0:T(1024)S(1)}, u32[]{:S(2)}, u32[]{:S(2)}) collective-permute-start(f32[4096]{0:T(1024)S(1)} %add.1096), channel_id=1, source_target_pairs={{4,36},{5,37},{6,38},{7,39},{12,44},{13,45},{14,46},{15,47},{20,52... | collective-permute-start | bytes 49160 | tf_op jit(solution)/shard_map/ppermute | solution.py:17
  305.4 4.5 %collective-permute-start.37 = (f32[4096]{0:T(1024)S(1)}, f32[4096]{0:T(1024)S(1)}, u32[]{:S(2)}, u32[]{:S(2)}) collective-permute-start(f32[4096]{0:T(1024)S(1)} %add.1099), channel_id=1, source_target_pairs={{4,12},{5,13},{6,14},{7,15},{12,4},{13,5},{14,6},{15,7},{20,28},{2... | collective-permute-start | bytes 49160 | tf_op jit(solution)/shard_map/ppermute | solution.py:17
  309.8 4.5 %collective-permute-start.38 = (f32[4096]{0:T(1024)S(1)}, f32[4096]{0:T(1024)S(1)}, u32[]{:S(2)}, u32[]{:S(2)}) collective-permute-start(f32[4096]{0:T(1024)S(1)} %add.1100), channel_id=1, source_target_pairs={{4,36},{5,37},{6,38},{7,39},{12,44},{13,45},{14,46},{15,47},{20,52... | collective-permute-start | bytes 49160 | tf_op jit(solution)/shard_map/ppermute | solution.py:17
  334.8 2.7 collective-permute-start.41
  337.5 4.5 %collective-permute-start.42 = (f32[4096]{0:T(1024)S(1)}, f32[4096]{0:T(1024)S(1)}, u32[]{:S(2)}, u32[]{:S(2)}) collective-permute-start(f32[4096]{0:T(1024)S(1)} %add.1103), channel_id=1, source_target_pairs={{4,12},{5,13},{6,14},{7,15},{12,4},{13,5},{14,6},{15,7},{20,28},{2... | collective-permute-start | bytes 49160 | tf_op jit(solution)/shard_map/ppermute | solution.py:17
  341.9 4.5 %collective-permute-start.43 = (f32[4096]{0:T(1024)S(1)}, f32[4096]{0:T(1024)S(1)}, u32[]{:S(2)}, u32[]{:S(2)}) collective-permute-start(f32[4096]{0:T(1024)S(1)} %add.1104), channel_id=1, source_target_pairs={{4,36},{5,37},{6,38},{7,39},{12,44},{13,45},{14,46},{15,47},{20,52... | collective-permute-start | bytes 49160 | tf_op jit(solution)/shard_map/ppermute | solution.py:17
  369.3 4.5 %collective-permute-start.47 = (f32[4096]{0:T(1024)S(1)}, f32[4096]{0:T(1024)S(1)}, u32[]{:S(2)}, u32[]{:S(2)}) collective-permute-start(f32[4096]{0:T(1024)S(1)} %add.1107), channel_id=1, source_target_pairs={{4,12},{5,13},{6,14},{7,15},{12,4},{13,5},{14,6},{15,7},{20,28},{2... | collective-permute-start | bytes 49160 | tf_op jit(solution)/shard_map/ppermute | solution.py:17
  373.8 4.5 %collective-permute-start.48 = (f32[4096]{0:T(1024)S(1)}, f32[4096]{0:T(1024)S(1)}, u32[]{:S(2)}, u32[]{:S(2)}) collective-permute-start(f32[4096]{0:T(1024)S(1)} %add.1108), channel_id=1, source_target_pairs={{4,36},{5,37},{6,38},{7,39},{12,44},{13,45},{14,46},{15,47},{20,52... | collective-permute-start | bytes 49160 | tf_op jit(solution)/shard_map/ppermute | solution.py:17
  378.3 3.0 collective-permute-start.49
  389.2 2.7 collective-permute-start.50
  400.4 8.3 %all-to-all-start.1 = ((bf16[4,2,2048]{2,1,0:T(2,128)(2,1)}), bf16[4,2,2048]{2,1,0:T(2,128)(2,1)S(1)}, u32[]{:S(2)}, u32[]{:S(2)}) async-start(bf16[4,2,2048]{2,1,0:T(2,128)(2,1)} %reshape.353), calls=%async_computation.1 | async-start | bytes 65536 | tf_op jit(solution)/shard_map/all_to_all | solution.py:181
  408.8 14.3 %all-to-all-start.2 = ((bf16[32,2,2048]{2,1,0:T(2,128)(2,1)}), bf16[32,2,2048]{2,1,0:T(2,128)(2,1)S(1)}, u32[]{:S(2)}, u32[]{:S(2)}) async-start(bf16[32,2,2048]{2,1,0:T(2,128)(2,1)} %reshape.355), calls=%async_computation.2 | async-start | bytes 524288 | tf_op jit(solution)/shard_map/all_to_all | solution.py:184
  (30 other events, 247.8 us)
